TPU v7x, 512 devices: a whole 4x8x8 slice. The times are simulated.
512 devices in a mesh: contact: 8 (over x, core), body: 8 (over z), group: 8 (over y).
Axes of the slice: x: 4, y: 8, z: 8, core: 2. Of those that a mesh axis runs over, the one named last changes fastest.
Arguments:
- jacobian_a: float32 [18, 1835008], P(None, ('contact', 'body', 'group')), may hold values from -4 to 4
- jacobian_b: float32 [18, 1835008], P(None, ('contact', 'body', 'group')), may hold values from -4 to 4
- warm_start: float32 [3, 1835008], P(None, ('contact', 'body', 'group')), may hold values from -4 to 4
- free_gap: float32 [3, 1835008], P(None, ('contact', 'body', 'group')), may hold values from -25 to 25
- compliance: float32 [3, 1835008], P(None, ('contact', 'body', 'group')), may hold values from 0.05 to 2.5
- friction: float32 [1835008], P(('contact', 'body', 'group')), may hold values from 0.2 to 0.8
- cone_active: int32 [1835008], P(('contact', 'body', 'group')), may hold values 0 or 1
- body_index_a: int32 [1835008], P(('contact', 'body', 'group')), may hold values from 0 to 4095
- body_index_b: int32 [1835008], P(('contact', 'body', 'group')), may hold values from 0 to 4095
- block_owner: int32 [28672, 1], P(('contact', 'body', 'group')), may hold values from 0 to 63; in each aligned block of 56 rows (0 to 55, 56 to 111, ...) at most 2 rows name the same one
- inverse_mass: float32 [6, 262144], P(None, ('body', 'group')), may hold values from 0.3 to 3
- free_velocity: float32 [6, 262144], P(None, ('body', 'group')), may hold values from -6 to 6
Outputs:
- impulse: float32 [3, 1835008], P(None, ('contact', 'body', 'group'))
- velocity: float32 [6, 262144], P(None, ('body', 'group'))
Inputs may be any that keep to these rules, and one draw needn't show every extreme that they name: `block_owner`: in each aligned block of 56 rows (the contact blocks of one device) no shard is named more than 2 times.
All inputs are finite; a program needn't handle non-finite values. No bound on the sum of `cone_active` on one device may be relied on, other than what follows from the above.
Results may differ from a plain program's by a relative error of at most 0.0003.
Values sent between devices are 32-bit elements; how exact they have to be, the bound alone decides.
A program may use at most 64 MiB of HBM per device.

v0:
```python
import math
import jax
import jax.numpy as jnp
from jax import lax
from jax.sharding import Mesh
from jax.sharding import PartitionSpec as P

CBLK = 64
ITERS = 2
CONTACT = ("contact_0", "contact_1")
CONTACT_BODY_GROUP = ("contact_0", "contact_1", "body", "group")
EPS = 1e-06
SMOOTH = 0.1


def copy_for_each(array, axis):
    length = lax.axis_size(axis)
    return lax.all_to_all(
        jnp.broadcast_to(array[None], (length, *array.shape)), axis, 0, 0, tiled=True
    )


def of_everyone(array, axis):
    everything = copy_for_each(array, axis)
    return jnp.sum(everything, axis=0)


def by_axis(array, axes):
    for axis in axes:
        array = lax.psum(array, axis)
    return array


def momentum_table(iterations):
    theta_now = 1.0
    coefficients = []
    for rounds in range(iterations):
        following = 0.5 * (
            theta_now * math.sqrt(theta_now * theta_now + 4.0) - theta_now * theta_now
        )
        coefficients.append(theta_now * (1.0 - theta_now) / (theta_now * theta_now + following))
        theta_now = following
    return coefficients


def project_cone(values, friction, cone_active):
    normal = values[0]
    tangent = values[1:3]
    spread = jnp.sqrt(tangent[0] * tangent[0] + tangent[1] * tangent[1] + SMOOTH * SMOOTH)
    sticking = spread <= friction * normal
    separated = friction * spread <= -normal
    cone_normal = (normal + friction * spread) / (1.0 + friction * friction)
    shrink_factor = friction * cone_normal / spread
    new_normal = jnp.where(sticking, normal, jnp.where(separated, 0.0, cone_normal))
    new_tangent = jnp.where(
        sticking[None], tangent, jnp.where(separated[None], 0.0, shrink_factor[None] * tangent)
    )
    switched = cone_active == 1
    out_normal = jnp.where(switched, new_normal, jnp.maximum(normal, 0.0))
    out_tangent = jnp.where(switched[None], new_tangent, 0.0)
    return jnp.concatenate([out_normal[None], out_tangent], axis=0)


def impulse_terms(jacobian, values):
    return jnp.sum(jacobian.reshape(3, 6, -1) * values[:, None, :], axis=0)


def velocity_terms(jacobian, velocities):
    return jnp.sum(jacobian.reshape(3, 6, -1) * velocities[None, :, :], axis=1)


def slot_places(block_owner, capacity):
    target = block_owner[:, 0]
    matching = (target[:, None] == target[None, :]).astype(jnp.int32)
    ordinal = jnp.arange(target.shape[0], dtype=jnp.int32)
    earlier = (ordinal[None, :] < ordinal[:, None]).astype(jnp.int32)
    ranking = jnp.sum(matching * earlier, axis=1)
    return target * capacity + ranking


def pack_slots(values, places, shards, capacity):
    leading = values.shape[0]
    blocks = values.reshape(leading, -1, CBLK)
    buffer = jnp.zeros((leading, shards * capacity, CBLK), values.dtype)
    buffer = buffer.at[:, places, :].set(blocks)
    return buffer.reshape(leading, shards, capacity * CBLK)


def unpack_slots(buffer, places):
    leading = buffer.shape[0]
    blocks = buffer.reshape(leading, -1, CBLK)[:, places, :]
    return blocks.reshape(leading, -1)


def trade(buffer):
    return lax.all_to_all(buffer, ("body", "group"), split_axis=1, concat_axis=1, tiled=True)


def on_device(
    jacobian_a,
    jacobian_b,
    warm_start,
    free_gap,
    compliance,
    friction,
    cone_active,
    body_index_a,
    body_index_b,
    block_owner,
    inverse_mass,
    free_velocity,
):
    shards = lax.axis_size(("body", "group"))
    capacity = max(2, 2 * block_owner.shape[0] // shards)
    places = slot_places(block_owner, capacity)
    bodies = inverse_mass.shape[1]
    index_slots = pack_slots(body_index_b[None, :], places, shards, capacity)
    far_index = lax.all_to_all(
        index_slots, ("body", "group"), split_axis=1, concat_axis=1, tiled=True
    ).reshape(-1)

    def body_impulse(values):
        summed = (
            jnp.zeros((6, bodies), jnp.float32)
            .at[:, body_index_a]
            .add(impulse_terms(jacobian_a, values))
        )
        far_terms = trade(
            pack_slots(impulse_terms(jacobian_b, values), places, shards, capacity)
        ).reshape(6, -1)
        summed = summed.at[:, far_index].add(far_terms)
        return of_everyone(summed, CONTACT)

    momentum = momentum_table(ITERS)
    current = warm_start
    before = jnp.zeros_like(warm_start)
    gradient_before = free_gap
    latest = warm_start
    for rounds in range(ITERS):
        velocities = inverse_mass * body_impulse(current)
        near_part = velocity_terms(jacobian_a, velocities[:, body_index_a])
        returned = trade(velocities[:, far_index].reshape(6, shards, -1))
        gradient = (
            near_part
            + velocity_terms(jacobian_b, unpack_slots(returned, places))
            + compliance * current
            + free_gap
        )
        iterate_change = current - before
        gradient_change = gradient - gradient_before
        change_squares, gradient_squares = (
            by_axis(jnp.sum(iterate_change * iterate_change), CONTACT_BODY_GROUP),
            by_axis(jnp.sum(gradient_change * gradient_change), CONTACT_BODY_GROUP),
        )
        stride = jnp.sqrt((change_squares + EPS) / (gradient_squares + EPS))
        projected = project_cone(current - stride * gradient, friction, cone_active)
        following = projected + momentum[rounds] * (projected - latest)
        before, gradient_before, latest, current = (current, gradient, projected, following)
    velocity = free_velocity + inverse_mass * body_impulse(latest)
    return (latest, velocity)


def solution(mesh):
    torus = Mesh(
        mesh.devices.reshape(4, 2, mesh.shape["body"], mesh.shape["group"]),
        ("contact_0", "contact_1", "body", "group"),
    )
    placed = (
        P(None, CONTACT_BODY_GROUP),
        P(None, CONTACT_BODY_GROUP),
        P(None, CONTACT_BODY_GROUP),
        P(None, CONTACT_BODY_GROUP),
        P(None, CONTACT_BODY_GROUP),
        P(CONTACT_BODY_GROUP),
        P(CONTACT_BODY_GROUP),
        P(CONTACT_BODY_GROUP),
        P(CONTACT_BODY_GROUP),
        P(CONTACT_BODY_GROUP, None),
        P(None, ("body", "group")),
        P(None, ("body", "group")),
    )
    return jax.shard_map(
        on_device,
        mesh=torus,
        in_specs=placed,
        out_specs=(P(None, CONTACT_BODY_GROUP), P(None, ("body", "group"))),
        check_vma=False,
    )
```

profile of v0, /device:TPU:8, one launch (start us, length us, event | category | flops | bytes accessed | tf_op | source)
XLA Modules:
  0.0 576.4 jit_solution(6024349499058837542)
XLA Ops:
  4.4 16.6 %all-to-all-start = ((s32[1,64,128]{2,0,1:T(1,128)}), s32[1,64,128]{2,0,1:T(1,128)S(1)}, u32[]{:S(2)}, u32[]{:S(2)}) async-start(s32[1,64,128]{2,0,1:T(1,128)} %bitcast.4), calls=%async_computation | async-start | bytes 65536 | tf_op jit(solution)/shard_map/all_to_all | solution.py:118
  30.2 20.5 %scatter_custom_fusion = f32[6,4096]{0,1:T(8,128)S(1)} fusion(s32[3584]{0:T(1024)S(1)} %compare_select_fusion.1, f32[3584,6]{1,0:T(8,128)} %copy.192, f32[]{:T(128)} %constant.10.clone.1), kind=kCustom, calls=%fused_computation.20 | custom fusion | flops 21504 | bytes 98816 | tf_op jit(solution)/shard_map/scatter-add | solution.py:126
  50.7 12.7 %all-to-all-start.1 = ((f32[6,64,128]{2,0,1:T(8,128)}), f32[6,64,128]{2,0,1:T(8,128)S(1)}, u32[]{:S(2)}, u32[]{:S(2)}) async-start(f32[6,64,128]{2,0,1:T(8,128)} %copy.196), calls=%async_computation.1 | async-start | bytes 524288 | tf_op jit(solution)/shard_map/all_to_all | solution.py:96
  63.5 13.7 %all-to-all-done.1 = f32[6,64,128]{2,0,1:T(8,128)S(1)} async-done(((f32[6,64,128]{2,0,1:T(8,128)}), f32[6,64,128]{2,0,1:T(8,128)S(1)}, u32[]{:S(2)}, u32[]{:S(2)}) %all-to-all-start.1) | async-done | bytes 196640 | tf_op jit(solution)/shard_map/all_to_all | solution.py:96
  79.8 51.8 %scatter_fusion.1 = f32[6,4096]{0,1:T(8,128)S(1)} fusion(f32[6,4096]{0,1:T(8,128)S(1)} %scatter_custom_fusion, s32[8192]{0:T(1024)S(1)} %bitcast.43, f32[8192,6]{1,0:T(8,128)} %copy.197), kind=kCustom, calls=%fused_computation.9 | custom fusion | flops 49152 | bytes 622592 | tf_op jit(solution)/shard_map/scatter-add | solution.py:131
  133.3 4.9 all-to-all-start.2
  138.2 16.0 %all-to-all-done.2 = f32[8,6,4096]{2,1,0:T(8,128)S(1)} async-done(((f32[8,6,4096]{2,1,0:T(8,128)}), f32[8,6,4096]{2,1,0:T(8,128)S(1)}, u32[]{:S(2)}, u32[]{:S(2)}) %all-to-all-start.2) | async-done | bytes 786464 | tf_op jit(solution)/shard_map/all_to_all | solution.py:18
  154.9 27.7 %gather_fusion.1 = f32[8192,6]{1,0:T(8,128)} fusion(f32[6,4096]{0,1:T(8,128)S(1)} %copy.200, s32[8192]{0:T(1024)S(1)} %broadcast_clamp_fusion), kind=kCustom, calls=%fused_computation.1 | custom fusion | bytes 425984 | tf_op jit(solution)/shard_map/gather | solution.py:142
  182.6 3.5 copy.203
  186.1 4.8 all-to-all-start.3
  191.0 7.3 %gather_fusion = f32[3584,6]{1,0:T(8,128)} fusion(f32[6,4096]{0,1:T(8,128)S(1)} %copy.200, s32[4096]{0:T(1024)S(1)} %pad_clamp_fusion), kind=kCustom, calls=%fused_computation | custom fusion | bytes 186368 | tf_op jit(solution)/shard_map/gather | solution.py:141
  200.4 4.7 all-to-all-done.3
  207.2 9.5 %all-reduce.5 = (f32[]{:T(128)}, f32[]{:T(128)}) all-reduce(f32[]{:T(128)} %get-tuple-element.40, f32[]{:T(128)} %get-tuple-element.38), channel_id=1, replica_groups=mesh['contact_0'=4,'contact_1'=2,'body'=8,'group'=8] {'contact_0'}, use_global_device_ids=true, to_apply=%region_1.0 | all-reduce | flops 2 | bytes 16 | tf_op jit(solution)/shard_map/psum | solution.py:30
  216.7 3.1 all-reduce.7
  219.8 15.4 %all-reduce.3 = (f32[]{:T(128)}, f32[]{:T(128)}) all-reduce(f32[]{:T(128)} %get-tuple-element.26, f32[]{:T(128)} %get-tuple-element.27), channel_id=1, replica_groups=mesh['contact_0'=4,'contact_1'=2,'body'=8,'group'=8] {'body'}, use_global_device_ids=true, to_apply=%region_3.0 | all-reduce | flops 2 | bytes 16 | tf_op jit(solution)/shard_map/psum | solution.py:30
  235.2 15.9 %all-reduce.1 = (f32[]{:T(128)}, f32[]{:T(128)}) all-reduce(f32[]{:T(128)} %get-tuple-element.18, f32[]{:T(128)} %get-tuple-element.19), channel_id=1, replica_groups=mesh['contact_0'=4,'contact_1'=2,'body'=8,'group'=8] {'group'}, use_global_device_ids=true, to_apply=%region_4.0 | all-reduce | flops 2 | bytes 16 | tf_op jit(solution)/shard_map/psum | solution.py:30
  257.2 8.2 %all-to-all-start.4 = ((f32[6,64,128]{2,0,1:T(8,128)}), f32[6,64,128]{2,0,1:T(8,128)S(1)}, u32[]{:S(2)}, u32[]{:S(2)}) async-start(f32[6,64,128]{2,0,1:T(8,128)} %copy.210), calls=%async_computation.4 | async-start | bytes 524288 | tf_op jit(solution)/shard_map/all_to_all | solution.py:96
  267.2 20.5 %scatter_custom_fusion.4 = f32[6,4096]{0,1:T(8,128)S(1)} fusion(s32[3584]{0:T(1024)S(1)} %compare_select_fusion.1, f32[3584,6]{1,0:T(8,128)} %copy.207, f32[]{:T(128)} %constant.10.clone.1), kind=kCustom, calls=%fused_computation.18 | custom fusion | flops 21504 | bytes 98816 | tf_op jit(solution)/shard_map/scatter-add | solution.py:126
  290.3 51.8 %scatter_fusion.3 = f32[6,4096]{0,1:T(8,128)S(1)} fusion(f32[6,4096]{0,1:T(8,128)S(1)} %scatter_custom_fusion.4, s32[8192]{0:T(1024)S(1)} %bitcast.45, f32[8192,6]{1,0:T(8,128)} %copy.211), kind=kCustom, calls=%fused_computation.12 | custom fusion | flops 49152 | bytes 622592 | tf_op jit(solution)/shard_map/scatter-add | solution.py:131
  342.8 18.8 %all_to_all.45 = f32[8,6,4096]{2,1,0:T(8,128)S(1)} all-to-all(f32[8,6,4096]{2,1,0:T(8,128)S(1)} %broadcast_in_dim.122), channel_id=1, replica_groups=mesh['contact_0'=4,'contact_1'=2,'body'=8,'group'=8] {'contact_0','conta..., dimensions={0} | all-to-all | bytes 1572864 | tf_op jit(solution)/shard_map/all_to_all | solution.py:18
  362.3 27.7 %gather_fusion.4 = f32[8192,6]{1,0:T(8,128)} fusion(f32[6,4096]{0,1:T(8,128)S(1)} %copy.214, s32[8192]{0:T(1024)S(1)} %broadcast_clamp_fusion), kind=kCustom, calls=%fused_computation.4 | custom fusion | bytes 425984 | tf_op jit(solution)/shard_map/gather | solution.py:142
  390.0 3.5 copy.217
  393.5 12.5 %all-to-all-start.6 = ((f32[6,64,128]{2,0,1:T(8,128)}), f32[6,64,128]{2,0,1:T(8,128)S(1)}, u32[]{:S(2)}, u32[]{:S(2)}) async-start(f32[6,64,128]{2,0,1:T(8,128)} %copy.217), calls=%async_computation.6 | async-start | bytes 524288 | tf_op jit(solution)/shard_map/all_to_all | solution.py:96
  406.0 7.3 %gather_fusion.3 = f32[3584,6]{1,0:T(8,128)} fusion(f32[6,4096]{0,1:T(8,128)S(1)} %copy.214, s32[4096]{0:T(1024)S(1)} %pad_clamp_fusion), kind=kCustom, calls=%fused_computation.3 | custom fusion | bytes 186368 | tf_op jit(solution)/shard_map/gather | solution.py:141
  415.5 4.4 all-to-all-done.6
  421.9 9.5 %all-reduce.4 = (f32[]{:T(128)}, f32[]{:T(128)}) all-reduce(f32[]{:T(128)} %get-tuple-element.33, f32[]{:T(128)} %get-tuple-element.31), channel_id=1, replica_groups=mesh['contact_0'=4,'contact_1'=2,'body'=8,'group'=8] {'contact_0'}, use_global_device_ids=true, to_apply=%region_21.22 | all-reduce | flops 2 | bytes 16 | tf_op jit(solution)/shard_map/psum | solution.py:30
  434.5 15.4 %all-reduce.2 = (f32[]{:T(128)}, f32[]{:T(128)}) all-reduce(f32[]{:T(128)} %get-tuple-element.24, f32[]{:T(128)} %get-tuple-element.25), channel_id=1, replica_groups=mesh['contact_0'=4,'contact_1'=2,'body'=8,'group'=8] {'body'}, use_global_device_ids=true, to_apply=%region_23.24 | all-reduce | flops 2 | bytes 16 | tf_op jit(solution)/shard_map/psum | solution.py:30
  449.9 15.9 %all-reduce = (f32[]{:T(128)}, f32[]{:T(128)}) all-reduce(f32[]{:T(128)} %get-tuple-element.16, f32[]{:T(128)} %get-tuple-element.17), channel_id=1, replica_groups=mesh['contact_0'=4,'contact_1'=2,'body'=8,'group'=8] {'group'}, use_global_device_ids=true, to_apply=%region_24.25 | all-reduce | flops 2 | bytes 16 | tf_op jit(solution)/shard_map/psum | solution.py:30
  471.3 8.2 %all-to-all-start.7 = ((f32[6,64,128]{2,0,1:T(8,128)}), f32[6,64,128]{2,0,1:T(8,128)S(1)}, u32[]{:S(2)}, u32[]{:S(2)}) async-start(f32[6,64,128]{2,0,1:T(8,128)} %copy.224), calls=%async_computation.7 | async-start | bytes 524288 | tf_op jit(solution)/shard_map/all_to_all | solution.py:96
  481.3 20.5 %scatter_custom_fusion.7 = f32[6,4096]{0,1:T(8,128)S(1)} fusion(s32[3584]{0:T(1024)S(1)} %compare_select_fusion.1, f32[3584,6]{1,0:T(8,128)} %copy.221, f32[]{:T(128)} %constant.10.clone.1), kind=kCustom, calls=%fused_computation.16 | custom fusion | flops 21504 | bytes 98816 | tf_op jit(solution)/shard_map/scatter-add | solution.py:126
  504.4 51.8 %scatter_fusion.5 = f32[6,4096]{0,1:T(8,128)S(1)} fusion(f32[6,4096]{0,1:T(8,128)S(1)} %scatter_custom_fusion.7, s32[8192]{0:T(1024)S(1)} %bitcast.46, f32[8192,6]{1,0:T(8,128)} %copy.225), kind=kCustom, calls=%fused_computation.15 | custom fusion | flops 49152 | bytes 622592 | tf_op jit(solution)/shard_map/scatter-add | solution.py:131
  556.9 18.7 %all_to_all.46 = f32[8,6,4096]{2,1,0:T(8,128)S(1)} all-to-all(f32[8,6,4096]{2,1,0:T(8,128)S(1)} %broadcast_in_dim.126), channel_id=1, replica_groups=mesh['contact_0'=4,'contact_1'=2,'body'=8,'group'=8] {'contact_0','conta..., dimensions={0} | all-to-all | bytes 1572864 | tf_op jit(solution)/shard_map/all_to_all | solution.py:18
  (108 shorter events, 49.8 us)
Async XLA Ops:
  4.4 46.3 %all-to-all-start = ((s32[1,64,128]{2,0,1:T(1,128)}), s32[1,64,128]{2,0,1:T(1,128)S(1)}, u32[]{:S(2)}, u32[]{:S(2)}) async-start(s32[1,64,128]{2,0,1:T(1,128)} %bitcast.4), calls=%async_computation | async-start | bytes 65536 | tf_op jit(solution)/shard_map/all_to_all | solution.py:118
  50.7 26.5 %all-to-all-start.1 = ((f32[6,64,128]{2,0,1:T(8,128)}), f32[6,64,128]{2,0,1:T(8,128)S(1)}, u32[]{:S(2)}, u32[]{:S(2)}) async-start(f32[6,64,128]{2,0,1:T(8,128)} %copy.196), calls=%async_computation.1 | async-start | bytes 524288 | tf_op jit(solution)/shard_map/all_to_all | solution.py:96
  132.3 22.0 %copy-start = (f32[6,4096]{1,0:T(8,128)S(1)}, f32[6,4096]{1,0:T(8,128)}, u32[]{:S(2)}) copy-start(f32[6,4096]{1,0:T(8,128)} %param.22) | copy-start | bytes 294916
  133.3 20.8 %all-to-all-start.2 = ((f32[8,6,4096]{2,1,0:T(8,128)}), f32[8,6,4096]{2,1,0:T(8,128)S(1)}, u32[]{:S(2)}, u32[]{:S(2)}) async-start(f32[8,6,4096]{2,1,0:T(8,128)} %broadcast_in_dim.66), calls=%async_computation.2 | async-start | bytes 2097152 | tf_op jit(solution)/shard_map/all_to_all | solution.py:18
  186.1 18.9 %all-to-all-start.3 = ((f32[6,64,128]{2,0,1:T(8,128)}), f32[6,64,128]{2,0,1:T(8,128)S(1)}, u32[]{:S(2)}, u32[]{:S(2)}) async-start(f32[6,64,128]{2,0,1:T(8,128)} %copy.203), calls=%async_computation.3 | async-start | bytes 524288 | tf_op jit(solution)/shard_map/all_to_all | solution.py:96
  200.4 6.1 %copy-start.1 = (f32[3,3584]{1,0:T(4,128)S(1)}, f32[3,3584]{1,0:T(4,128)}, u32[]{:S(2)}) copy-start(f32[3,3584]{1,0:T(4,128)} %param.14) | copy-start | bytes 129028
  200.4 6.1 %copy-start.2 = (f32[3,3584]{1,0:T(4,128)S(1)}, f32[3,3584]{1,0:T(4,128)}, u32[]{:S(2)}) copy-start(f32[3,3584]{1,0:T(4,128)} %param.15) | copy-start | bytes 129028
  200.4 6.2 %copy-start.3 = (f32[3,3584]{1,0:T(4,128)S(1)}, f32[3,3584]{1,0:T(4,128)}, u32[]{:S(2)}) copy-start(f32[3,3584]{1,0:T(4,128)} %param.16) | copy-start | bytes 129028
  205.1 47.5 %copy-start.5 = (f32[3584]{0:T(1024)S(1)}, f32[3584]{0:T(1024)}, u32[]{:S(2)}) copy-start(f32[3584]{0:T(1024)} %param.17) | copy-start | bytes 43012
  205.1 47.5 %copy-start.7 = (s32[3584]{0:T(1024)S(1)}, s32[3584]{0:T(1024)}, u32[]{:S(2)}) copy-start(s32[3584]{0:T(1024)} %param.18) | copy-start | bytes 43012
  257.2 30.5 %all-to-all-start.4 = ((f32[6,64,128]{2,0,1:T(8,128)}), f32[6,64,128]{2,0,1:T(8,128)S(1)}, u32[]{:S(2)}, u32[]{:S(2)}) async-start(f32[6,64,128]{2,0,1:T(8,128)} %copy.210), calls=%async_computation.4 | async-start | bytes 524288 | tf_op jit(solution)/shard_map/all_to_all | solution.py:96
  393.5 26.5 %all-to-all-start.6 = ((f32[6,64,128]{2,0,1:T(8,128)}), f32[6,64,128]{2,0,1:T(8,128)S(1)}, u32[]{:S(2)}, u32[]{:S(2)}) async-start(f32[6,64,128]{2,0,1:T(8,128)} %copy.217), calls=%async_computation.6 | async-start | bytes 524288 | tf_op jit(solution)/shard_map/all_to_all | solution.py:96
  467.5 3.0 copy-start.4
  471.3 30.5 %all-to-all-start.7 = ((f32[6,64,128]{2,0,1:T(8,128)}), f32[6,64,128]{2,0,1:T(8,128)S(1)}, u32[]{:S(2)}, u32[]{:S(2)}) async-start(f32[6,64,128]{2,0,1:T(8,128)} %copy.224), calls=%async_computation.7 | async-start | bytes 524288 | tf_op jit(solution)/shard_map/all_to_all | solution.py:96
  556.8 18.9 %copy-start.6 = (f32[6,4096]{1,0:T(8,128)S(1)}, f32[6,4096]{1,0:T(8,128)}, u32[]{:S(2)}) copy-start(f32[6,4096]{1,0:T(8,128)} %param.23) | copy-start | bytes 294916
where the time goes:
time: 578 us; the launch traced here: 576 us
  other arithmetic  224 us (39%)
  blocking collectives  125 us (22%)
  local copies, waits for them, and re-layouts  116 us (20%)
  starting transfers between devices  67.9 us (12%)
  waiting for transfers between devices  38.8 us (7%)
    scatter-add x3, other arithmetic, body_impulse(): summed = summed.at[:, far_index].add(far_terms)  155 us
    psum x8, blocking collectives, by_axis(): array = lax.psum(array, axis)  87.7 us
    scatter-add x3, other arithmetic, body_impulse(): summed = jnp.zeros((6, bodies), jnp.float32).at[:, body_index_a].add(impu...  61.4 us
    gather x2, local copies, waits for them, and re-layouts, on_device(): returned = trade(velocities[:, far_index].reshape(6, shards, -1))  55.4 us
    all_to_all x5, starting transfers between devices, trade(): lax.all_to_all(buffer, ('body', 'group'), split_axis=1, concat_axis=1, ti...  46.4 us
    all_to_all x2, blocking collectives, copy_for_each(): lax.all_to_all(jnp.broadcast_to(array[None], (length, *array.shape)), axi...  37.5 us
    all_to_all x5, waiting for transfers between devices, trade(): lax.all_to_all(buffer, ('body', 'group'), split_axis=1, concat_axis=1, ti...  22.8 us
    gather x4, local copies, waits for them, and re-layouts, on_device(): near_part = velocity_terms(jacobian_a, velocities[:, body_index_a])  18.8 us
  transfers between devices with their start and end apart: 7, of which 4 were waited for; matrix products, arithmetic and copies ran while one was open for 16% of the time, Pallas kernels for 0%

commit v1 on v0

--- a/solution.py
+++ b/solution.py
@@ -27,7 +27,7 @@
 
 def by_axis(array, axes):
     for axis in axes:
-        array = lax.psum(array, axis)
+        array = jnp.sum(lax.all_gather(array, axis), axis=0)
     return array
 
 

time: 578 us -> 609 us (1.054)
  local copies, waits for them, and re-layouts: 116 us -> 144 us
  other arithmetic: 224 us -> 234 us
    psum x8 -> x0, blocking collectives: 87.7 us -> none  [by_axis(): array = lax.psum(array, axis)]
    unnamed x0 -> x8, blocking collectives: none -> 82.6 us
    unnamed x16 -> x52, local copies, waits for them, and re-layouts: 0.04 us -> 27.6 us
    reduce_sum x0 -> x16, other arithmetic: none -> 9.87 us  [by_axis(): array = jnp.sum(lax.all_gather(array, axis), axis=0)]
where the time goes in v1:
time: 609 us; the launch traced here: 608 us
  other arithmetic  234 us (38%)
  local copies, waits for them, and re-layouts  144 us (24%)
  blocking collectives  120 us (20%)
  starting transfers between devices  69.6 us (11%)
  waiting for transfers between devices  36.2 us (6%)
    scatter-add x3, other arithmetic, body_impulse(): summed = summed.at[:, far_index].add(far_terms)  155 us
    unnamed x8, blocking collectives  82.6 us
    scatter-add x3, other arithmetic, body_impulse(): summed = jnp.zeros((6, bodies), jnp.float32).at[:, body_index_a].add(impu...  61.4 us
    gather x2, local copies, waits for them, and re-layouts, on_device(): returned = trade(velocities[:, far_index].reshape(6, shards, -1))  55.4 us
    all_to_all x5, starting transfers between devices, trade(): lax.all_to_all(buffer, ('body', 'group'), split_axis=1, concat_axis=1, ti...  48.1 us
    all_to_all x2, blocking collectives, copy_for_each(): lax.all_to_all(jnp.broadcast_to(array[None], (length, *array.shape)), axi...  37.5 us
    unnamed x52, local copies, waits for them, and re-layouts  27.6 us
    all_to_all x5, waiting for transfers between devices, trade(): lax.all_to_all(buffer, ('body', 'group'), split_axis=1, concat_axis=1, ti...  20.2 us
  transfers between devices with their start and end apart: 7, of which 4 were waited for; matrix products, arithmetic and copies ran while one was open for 16% of the time, Pallas kernels for 0%

profile of v1, /device:TPU:8, one launch (start us, length us, event | category | flops | bytes accessed | tf_op | source)
XLA Modules:
  0.0 607.9 jit_solution(851980700607022573)
XLA Ops:
  4.4 16.6 %all-to-all-start = ((s32[1,64,128]{2,0,1:T(1,128)}), s32[1,64,128]{2,0,1:T(1,128)S(1)}, u32[]{:S(2)}, u32[]{:S(2)}) async-start(s32[1,64,128]{2,0,1:T(1,128)} %bitcast.12), calls=%async_computation | async-start | bytes 65536 | tf_op jit(solution)/shard_map/all_to_all | solution.py:118
  30.2 20.5 %scatter_custom_fusion = f32[6,4096]{0,1:T(8,128)S(1)} fusion(s32[3584]{0:T(1024)S(1)} %compare_select_fusion.1, f32[3584,6]{1,0:T(8,128)} %copy.192, f32[]{:T(128)} %constant.10.clone.1), kind=kCustom, calls=%fused_computation.20 | custom fusion | flops 21504 | bytes 98816 | tf_op jit(solution)/shard_map/scatter-add | solution.py:126
  50.7 12.7 %all-to-all-start.1 = ((f32[6,64,128]{2,0,1:T(8,128)}), f32[6,64,128]{2,0,1:T(8,128)S(1)}, u32[]{:S(2)}, u32[]{:S(2)}) async-start(f32[6,64,128]{2,0,1:T(8,128)} %copy.196), calls=%async_computation.1 | async-start | bytes 524288 | tf_op jit(solution)/shard_map/all_to_all | solution.py:96
  63.5 13.7 %all-to-all-done.1 = f32[6,64,128]{2,0,1:T(8,128)S(1)} async-done(((f32[6,64,128]{2,0,1:T(8,128)}), f32[6,64,128]{2,0,1:T(8,128)S(1)}, u32[]{:S(2)}, u32[]{:S(2)}) %all-to-all-start.1) | async-done | bytes 196640 | tf_op jit(solution)/shard_map/all_to_all | solution.py:96
  79.8 51.8 %scatter_fusion.1 = f32[6,4096]{0,1:T(8,128)S(1)} fusion(f32[6,4096]{0,1:T(8,128)S(1)} %scatter_custom_fusion, s32[8192]{0:T(1024)S(1)} %bitcast.63, f32[8192,6]{1,0:T(8,128)} %copy.197), kind=kCustom, calls=%fused_computation.9 | custom fusion | flops 49152 | bytes 622592 | tf_op jit(solution)/shard_map/scatter-add | solution.py:131
  133.3 4.9 all-to-all-start.2
  138.2 16.0 %all-to-all-done.2 = f32[8,6,4096]{2,1,0:T(8,128)S(1)} async-done(((f32[8,6,4096]{2,1,0:T(8,128)}), f32[8,6,4096]{2,1,0:T(8,128)S(1)}, u32[]{:S(2)}, u32[]{:S(2)}) %all-to-all-start.2) | async-done | bytes 786464 | tf_op jit(solution)/shard_map/all_to_all | solution.py:18
  154.9 27.7 %gather_fusion.1 = f32[8192,6]{1,0:T(8,128)} fusion(f32[6,4096]{0,1:T(8,128)S(1)} %copy.200, s32[8192]{0:T(1024)S(1)} %broadcast_clamp_fusion), kind=kCustom, calls=%fused_computation.1 | custom fusion | bytes 425984 | tf_op jit(solution)/shard_map/gather | solution.py:142
  182.6 3.5 copy.203
  186.1 4.8 all-to-all-start.3
  192.2 7.3 %gather_fusion = f32[3584,6]{1,0:T(8,128)} fusion(f32[6,4096]{0,1:T(8,128)S(1)} %copy.200, s32[4096]{0:T(1024)S(1)} %pad_clamp_fusion), kind=kCustom, calls=%fused_computation | custom fusion | bytes 186368 | tf_op jit(solution)/shard_map/gather | solution.py:141
  201.6 3.4 all-to-all-done.3
  211.1 8.9 %all-reduce.21 = (f32[4]{0:T(128)S(1)}, f32[4]{0:T(128)S(1)}) all-reduce(f32[4]{0:T(128)S(1)} %dynamic-update-slice, f32[4]{0:T(128)S(1)} %dynamic-update-slice.4), channel_id=1, replica_groups=mesh['contact_0'=4,'contact_1'=2,'body'=8,'group'=8] {'contact_0'}, use_global_device_ids=true, to_apply=%add | all-reduce | flops 8 | bytes 64
  233.4 14.8 %all-reduce.19 = (f32[8]{0:T(128)S(1)}, f32[8]{0:T(128)S(1)}) all-reduce(f32[8]{0:T(128)S(1)} %dynamic-update-slice.2, f32[8]{0:T(128)S(1)} %dynamic-update-slice.6), channel_id=1, replica_groups=mesh['contact_0'=4,'contact_1'=2,'body'=8,'group'=8] {'body'}, use_global_device_ids=true, to_apply=%add.2 | all-reduce | flops 16 | bytes 128
  252.3 15.3 %all-reduce.17 = (f32[8]{0:T(128)S(1)}, f32[8]{0:T(128)S(1)}) all-reduce(f32[8]{0:T(128)S(1)} %dynamic-update-slice.3, f32[8]{0:T(128)S(1)} %dynamic-update-slice.7), channel_id=1, replica_groups=mesh['contact_0'=4,'contact_1'=2,'body'=8,'group'=8] {'group'}, use_global_device_ids=true, to_apply=%add.3 | all-reduce | flops 16 | bytes 128
  274.9 8.8 %all-to-all-start.4 = ((f32[6,64,128]{2,0,1:T(8,128)}), f32[6,64,128]{2,0,1:T(8,128)S(1)}, u32[]{:S(2)}, u32[]{:S(2)}) async-start(f32[6,64,128]{2,0,1:T(8,128)} %copy.210), calls=%async_computation.4 | async-start | bytes 524288 | tf_op jit(solution)/shard_map/all_to_all | solution.py:96
  285.5 20.5 %scatter_custom_fusion.4 = f32[6,4096]{0,1:T(8,128)S(1)} fusion(s32[3584]{0:T(1024)S(1)} %compare_select_fusion.1, f32[3584,6]{1,0:T(8,128)} %copy.207, f32[]{:T(128)} %constant.10.clone.1), kind=kCustom, calls=%fused_computation.18 | custom fusion | flops 21504 | bytes 98816 | tf_op jit(solution)/shard_map/scatter-add | solution.py:126
  305.9 2.6 copy.211
  308.6 51.8 %scatter_fusion.3 = f32[6,4096]{0,1:T(8,128)S(1)} fusion(f32[6,4096]{0,1:T(8,128)S(1)} %scatter_custom_fusion.4, s32[8192]{0:T(1024)S(1)} %bitcast.65, f32[8192,6]{1,0:T(8,128)} %copy.211), kind=kCustom, calls=%fused_computation.12 | custom fusion | flops 49152 | bytes 622592 | tf_op jit(solution)/shard_map/scatter-add | solution.py:131
  361.1 18.8 %all_to_all.45 = f32[8,6,4096]{2,1,0:T(8,128)S(1)} all-to-all(f32[8,6,4096]{2,1,0:T(8,128)S(1)} %broadcast_in_dim.122), channel_id=1, replica_groups=mesh['contact_0'=4,'contact_1'=2,'body'=8,'group'=8] {'contact_0','conta..., dimensions={0} | all-to-all | bytes 1572864 | tf_op jit(solution)/shard_map/all_to_all | solution.py:18
  380.6 27.7 %gather_fusion.4 = f32[8192,6]{1,0:T(8,128)} fusion(f32[6,4096]{0,1:T(8,128)S(1)} %copy.214, s32[8192]{0:T(1024)S(1)} %broadcast_clamp_fusion), kind=kCustom, calls=%fused_computation.4 | custom fusion | bytes 425984 | tf_op jit(solution)/shard_map/gather | solution.py:142
  408.3 3.5 copy.217
  411.8 12.7 %all-to-all-start.6 = ((f32[6,64,128]{2,0,1:T(8,128)}), f32[6,64,128]{2,0,1:T(8,128)S(1)}, u32[]{:S(2)}, u32[]{:S(2)}) async-start(f32[6,64,128]{2,0,1:T(8,128)} %copy.217), calls=%async_computation.6 | async-start | bytes 524288 | tf_op jit(solution)/shard_map/all_to_all | solution.py:96
  425.8 7.3 %gather_fusion.3 = f32[3584,6]{1,0:T(8,128)} fusion(f32[6,4096]{0,1:T(8,128)S(1)} %copy.214, s32[4096]{0:T(1024)S(1)} %pad_clamp_fusion), kind=kCustom, calls=%fused_computation.3 | custom fusion | bytes 186368 | tf_op jit(solution)/shard_map/gather | solution.py:141
  435.4 3.1 all-to-all-done.6
  441.8 8.9 %all-reduce.20 = (f32[4]{0:T(128)S(1)}, f32[4]{0:T(128)S(1)}) all-reduce(f32[4]{0:T(128)S(1)} %dynamic-update-slice.8, f32[4]{0:T(128)S(1)} %dynamic-update-slice.12), channel_id=1, replica_groups=mesh['contact_0'=4,'contact_1'=2,'body'=8,'group'=8] {'contact_0'}, use_global_device_ids=true, to_apply=%add.8 | all-reduce | flops 8 | bytes 64
  461.2 14.8 %all-reduce.18 = (f32[8]{0:T(128)S(1)}, f32[8]{0:T(128)S(1)}) all-reduce(f32[8]{0:T(128)S(1)} %dynamic-update-slice.10, f32[8]{0:T(128)S(1)} %dynamic-update-slice.14), channel_id=1, replica_groups=mesh['contact_0'=4,'contact_1'=2,'body'=8,'group'=8] {'body'}, use_global_device_ids=true, to_apply=%add.10 | all-reduce | flops 16 | bytes 128
  479.9 15.2 %all-reduce.16 = (f32[8]{0:T(128)S(1)}, f32[8]{0:T(128)S(1)}) all-reduce(f32[8]{0:T(128)S(1)} %dynamic-update-slice.11, f32[8]{0:T(128)S(1)} %dynamic-update-slice.15), channel_id=1, replica_groups=mesh['contact_0'=4,'contact_1'=2,'body'=8,'group'=8] {'group'}, use_global_device_ids=true, to_apply=%add.11 | all-reduce | flops 16 | bytes 128
  501.8 9.1 %all-to-all-start.7 = ((f32[6,64,128]{2,0,1:T(8,128)}), f32[6,64,128]{2,0,1:T(8,128)S(1)}, u32[]{:S(2)}, u32[]{:S(2)}) async-start(f32[6,64,128]{2,0,1:T(8,128)} %copy.224), calls=%async_computation.7 | async-start | bytes 524288 | tf_op jit(solution)/shard_map/all_to_all | solution.py:96
  512.8 20.5 %scatter_custom_fusion.7 = f32[6,4096]{0,1:T(8,128)S(1)} fusion(s32[3584]{0:T(1024)S(1)} %compare_select_fusion.1, f32[3584,6]{1,0:T(8,128)} %copy.221, f32[]{:T(128)} %constant.10.clone.1), kind=kCustom, calls=%fused_computation.16 | custom fusion | flops 21504 | bytes 98816 | tf_op jit(solution)/shard_map/scatter-add | solution.py:126
  535.9 51.8 %scatter_fusion.5 = f32[6,4096]{0,1:T(8,128)S(1)} fusion(f32[6,4096]{0,1:T(8,128)S(1)} %scatter_custom_fusion.7, s32[8192]{0:T(1024)S(1)} %bitcast.66, f32[8192,6]{1,0:T(8,128)} %copy.225), kind=kCustom, calls=%fused_computation.15 | custom fusion | flops 49152 | bytes 622592 | tf_op jit(solution)/shard_map/scatter-add | solution.py:131
  588.4 18.7 %all_to_all.46 = f32[8,6,4096]{2,1,0:T(8,128)S(1)} all-to-all(f32[8,6,4096]{2,1,0:T(8,128)S(1)} %broadcast_in_dim.126), channel_id=1, replica_groups=mesh['contact_0'=4,'contact_1'=2,'body'=8,'group'=8] {'contact_0','conta..., dimensions={0} | all-to-all | bytes 1572864 | tf_op jit(solution)/shard_map/all_to_all | solution.py:18
  (160 shorter events, 86.4 us)
Async XLA Ops:
  4.4 46.3 %all-to-all-start = ((s32[1,64,128]{2,0,1:T(1,128)}), s32[1,64,128]{2,0,1:T(1,128)S(1)}, u32[]{:S(2)}, u32[]{:S(2)}) async-start(s32[1,64,128]{2,0,1:T(1,128)} %bitcast.12), calls=%async_computation | async-start | bytes 65536 | tf_op jit(solution)/shard_map/all_to_all | solution.py:118
  50.7 26.5 %all-to-all-start.1 = ((f32[6,64,128]{2,0,1:T(8,128)}), f32[6,64,128]{2,0,1:T(8,128)S(1)}, u32[]{:S(2)}, u32[]{:S(2)}) async-start(f32[6,64,128]{2,0,1:T(8,128)} %copy.196), calls=%async_computation.1 | async-start | bytes 524288 | tf_op jit(solution)/shard_map/all_to_all | solution.py:96
  132.3 22.0 %copy-start = (f32[6,4096]{1,0:T(8,128)S(1)}, f32[6,4096]{1,0:T(8,128)}, u32[]{:S(2)}) copy-start(f32[6,4096]{1,0:T(8,128)} %param.22) | copy-start | bytes 294916
  133.3 20.8 %all-to-all-start.2 = ((f32[8,6,4096]{2,1,0:T(8,128)}), f32[8,6,4096]{2,1,0:T(8,128)S(1)}, u32[]{:S(2)}, u32[]{:S(2)}) async-start(f32[8,6,4096]{2,1,0:T(8,128)} %broadcast_in_dim.66), calls=%async_computation.2 | async-start | bytes 2097152 | tf_op jit(solution)/shard_map/all_to_all | solution.py:18
  186.1 18.9 %all-to-all-start.3 = ((f32[6,64,128]{2,0,1:T(8,128)}), f32[6,64,128]{2,0,1:T(8,128)S(1)}, u32[]{:S(2)}, u32[]{:S(2)}) async-start(f32[6,64,128]{2,0,1:T(8,128)} %copy.203), calls=%async_computation.3 | async-start | bytes 524288 | tf_op jit(solution)/shard_map/all_to_all | solution.py:96
  201.6 4.9 copy-start.1
  201.6 4.9 copy-start.2
  201.6 4.9 copy-start.3
  205.1 65.2 %copy-start.5 = (f32[3584]{0:T(1024)S(1)}, f32[3584]{0:T(1024)}, u32[]{:S(2)}) copy-start(f32[3584]{0:T(1024)} %param.17) | copy-start | bytes 43012
  205.1 65.2 %copy-start.7 = (s32[3584]{0:T(1024)S(1)}, s32[3584]{0:T(1024)}, u32[]{:S(2)}) copy-start(s32[3584]{0:T(1024)} %param.18) | copy-start | bytes 43012
  274.9 31.1 %all-to-all-start.4 = ((f32[6,64,128]{2,0,1:T(8,128)}), f32[6,64,128]{2,0,1:T(8,128)S(1)}, u32[]{:S(2)}, u32[]{:S(2)}) async-start(f32[6,64,128]{2,0,1:T(8,128)} %copy.210), calls=%async_computation.4 | async-start | bytes 524288 | tf_op jit(solution)/shard_map/all_to_all | solution.py:96
  411.8 26.7 %all-to-all-start.6 = ((f32[6,64,128]{2,0,1:T(8,128)}), f32[6,64,128]{2,0,1:T(8,128)S(1)}, u32[]{:S(2)}, u32[]{:S(2)}) async-start(f32[6,64,128]{2,0,1:T(8,128)} %copy.217), calls=%async_computation.6 | async-start | bytes 524288 | tf_op jit(solution)/shard_map/all_to_all | solution.py:96
  498.0 3.0 copy-start.4
  501.8 31.4 %all-to-all-start.7 = ((f32[6,64,128]{2,0,1:T(8,128)}), f32[6,64,128]{2,0,1:T(8,128)S(1)}, u32[]{:S(2)}, u32[]{:S(2)}) async-start(f32[6,64,128]{2,0,1:T(8,128)} %copy.224), calls=%async_computation.7 | async-start | bytes 524288 | tf_op jit(solution)/shard_map/all_to_all | solution.py:96
  588.3 18.9 %copy-start.6 = (f32[6,4096]{1,0:T(8,128)S(1)}, f32[6,4096]{1,0:T(8,128)}, u32[]{:S(2)}) copy-start(f32[6,4096]{1,0:T(8,128)} %param.23) | copy-start | bytes 294916
